TPU v7x, 32 devices: a whole 2x2x4 slice. The times are simulated.
32 devices in a mesh: group: 4 (over y, core), member: 8 (over z, x).
Axes of the slice: x: 2, y: 2, z: 4, core: 2. Of those that a mesh axis runs over, the one named last changes fastest.
Arguments:
- tokens: bfloat16 [128, 196, 768], P(('group', 'member')), may hold values from -6 to 6
- w_query: bfloat16 [768, 768], replicated, may hold values from -8 to 8
- w_key: bfloat16 [768, 768], replicated, may hold values from -1 to 1
- w_value: bfloat16 [768, 768], replicated, may hold values from -0.21875 to 0.21875
- w_out: bfloat16 [768, 768], replicated, may hold values from -0.21875 to 0.21875
- partners: int32 [128, 4], P(('group', 'member')), may hold values from 0 to 127, as said below
- counts: int32 [128], P(('group', 'member')), may hold values from 1 to 4
- key_slot: int32 [32], P(('group', 'member')), may hold values from 0 to 3
Outputs:
- refined: bfloat16 [128, 196, 768], P(('group', 'member'))
Inputs may be any that keep to these rules, and one draw needn't show every extreme that they name: `partners`: every entry names a view held by another device of the same group; the entries of all views of one device name views of one other device at most 3 times, and those of some other device exactly 3 times.
All inputs are finite; a program needn't handle non-finite values.
Results may differ from a plain program's by a relative error of at most 0.011.
Values may be sent and summed in bfloat16 or wider, within the bound.
A program may use at most 128 MiB of HBM per device.

v0:
```python
import functools

import jax
import jax.numpy as jnp
from jax import lax
from jax.experimental import pallas as pl
from jax.experimental.pallas import tpu as pltpu
from jax.experimental.layout import Layout, with_layout_constraint
from jax.sharding import PartitionSpec as P


HEADS = 12
ROW = 2


def layer_norm(values_in):
    values_in = values_in.astype(jnp.float32)
    centre = jnp.mean(values_in, axis=-1, keepdims=True)
    spread = jnp.mean((values_in - centre) ** 2, axis=-1, keepdims=True)
    return (values_in - centre) * lax.rsqrt(spread + 1e-05)


def step_kernel(phase, first, final, places, *refs):
    table, queries, w_key, w_value = refs[:4]
    blocks = refs[4 : 4 + len(places)]
    rest = list(refs[4 + len(places) :])
    if not first:
        total_in = rest.pop(0)
    if final:
        inverse, tokens, w_out = rest[:3]
        rest = rest[3:]
    out_ref = rest.pop(0)
    held, pair, total, sems = rest
    copies = [
        pltpu.make_async_copy(block, held.at[pl.ds(place, block.shape[0])], sems.at[i])
        for i, (place, block) in enumerate(zip(places, blocks))
    ]
    if not first:
        copies.append(pltpu.make_async_copy(total_in, total, sems.at[len(copies)]))
    for copy in copies:
        copy.start()
    if first:
        total[...] = jnp.zeros_like(total)
    for copy in copies:
        copy.wait()
    views, _, features = queries.shape
    size = features // HEADS
    lanes = lax.broadcasted_iota(jnp.int32, (1, 2 * size), 1)
    lower = lanes < size

    def entry(e, carry):
        @pl.when(table[0, e] == phase)
        def _():
            place, view = table[1, e], table[2, e]
            normed = layer_norm(held[place]).astype(jnp.bfloat16)
            pair[:, :features] = jnp.dot(
                normed, w_key[...], preferred_element_type=jnp.float32
            ).astype(jnp.bfloat16)
            pair[:, features:] = jnp.dot(
                normed, w_value[...], preferred_element_type=jnp.float32
            ).astype(jnp.bfloat16)
            for h in range(HEADS // 2):
                cols = pl.ds(2 * h * size, 2 * size)
                query = queries[view, :, cols] * jnp.bfloat16(size**-0.5)
                key = pair[:, cols]
                value = pair[:, pl.ds(features + 2 * h * size, 2 * size)]
                halves = []
                for keep in (lower, jnp.logical_not(lower)):
                    part = jnp.where(keep, query, jnp.zeros_like(query))
                    scores = lax.dot_general(
                        part, key, (((1,), (1,)), ((), ())), preferred_element_type=jnp.float32
                    )
                    top = jnp.max(scores, axis=-1, keepdims=True)
                    weights = jnp.exp(scores - top)
                    mass = jnp.sum(weights, axis=-1, keepdims=True)
                    result = jnp.dot(
                        weights.astype(jnp.bfloat16), value, preferred_element_type=jnp.float32
                    )
                    halves.append(result / mass)
                total[view, :, cols] += jnp.where(lower, halves[0], halves[1])

        return carry

    lax.fori_loop(0, table.shape[1], entry, 0)
    if final:
        for v in range(views):
            mixed = (total[v] * inverse[v]).astype(jnp.bfloat16)
            projected = jnp.dot(mixed, w_out[...], preferred_element_type=jnp.float32)
            out_ref[v] = (tokens[v].astype(jnp.float32) + projected).astype(out_ref.dtype)
    else:
        copy = pltpu.make_async_copy(total, out_ref, sems.at[0])
        copy.start()
        copy.wait()


def add_phase(phase, table, queries, w_key, w_value, blocks, total, finish=None):
    views, length, features = queries.shape
    first, final = total is None, finish is not None
    places = [place for place, _ in blocks]
    arrays = [block for _, block in blocks]
    depth = max(place + block.shape[0] for place, block in blocks)
    vmem = pl.BlockSpec(memory_space=pltpu.VMEM)
    smem = pl.BlockSpec(memory_space=pltpu.SMEM)
    hbm = pl.BlockSpec(memory_space=pl.ANY)
    operands = [table, queries, w_key, w_value, *arrays]
    specs = [smem, vmem, vmem, vmem] + [hbm] * len(arrays)
    if not first:
        operands.append(total)
        specs.append(hbm)
    if final:
        operands += list(finish)
        specs += [smem, vmem, vmem]
    entries = 4
    return pl.pallas_call(
        functools.partial(step_kernel, phase, first, final, places),
        out_shape=jax.ShapeDtypeStruct(
            queries.shape, jnp.bfloat16 if final else jnp.float32
        ),
        in_specs=specs,
        out_specs=vmem if final else hbm,
        scratch_shapes=[
            pltpu.VMEM((depth, length, features), jnp.bfloat16),
            pltpu.VMEM((length, 2 * features), jnp.bfloat16),
            pltpu.VMEM((views, length, features), jnp.float32),
            pltpu.SemaphoreType.DMA((len(arrays) + 1,)),
        ],
        compiler_params=pltpu.CompilerParams(vmem_limit_bytes=56 * 1024 * 1024),
        cost_estimate=pl.CostEstimate(
            flops=entries * length * features * (4 * features + 4 * 4 * length),
            bytes_accessed=8 * views * length * features,
            transcendentals=entries * HEADS * length * length,
        ),
        name="attend_phase",
    )(*operands)


def pick(block, indices):
    def copy_view(index_ref, source, target):
        target[...] = source[...]

    shape = (1,) + block.shape[1:]
    return pl.pallas_call(
        copy_view,
        grid_spec=pltpu.PrefetchScalarGridSpec(
            num_scalar_prefetch=1,
            grid=indices.shape,
            in_specs=[pl.BlockSpec(shape, lambda i, index: (index[i], 0, 0))],
            out_specs=pl.BlockSpec(shape, lambda i, index: (i, 0, 0)),
        ),
        out_shape=jax.ShapeDtypeStruct(indices.shape + block.shape[1:], block.dtype),
        name="pick_views",
    )(indices, block)


def sublayer(tokens, w_query, w_key, w_value, w_out, partners, counts, key_slot):
    views_here, length, features = tokens.shape
    tokens = with_layout_constraint(tokens, Layout(major_to_minor=(0, 1, 2)))
    members = lax.axis_size("member")
    groups = lax.axis_size("group")
    me = lax.axis_index("member")
    degree = partners.shape[1]
    slot_key = key_slot[0]
    entry_list = partners.reshape(-1)
    entry_count = entry_list.shape[0]
    capacity = (entry_count + members - 2) // (members - 1)
    peers = entry_list // views_here % members
    places = entry_list % views_here
    order = jnp.arange(entry_count, dtype=jnp.int32)
    same_peer = (peers[:, None] == peers[None, :]) & (order[None, :] < order[:, None])
    ranks = jnp.sum(same_peer.astype(jnp.int32), axis=1)
    live = (jnp.arange(degree, dtype=jnp.int32)[None, :] < counts[:, None]).reshape(-1)
    entry_views = order // degree
    gather = members * views_here <= 2 * entry_count and members % ROW == 0

    def keyframes(after=None):
        slot = slot_key if after is None else lax.optimization_barrier((slot_key, after))[0]
        own_key = lax.dynamic_slice_in_dim(tokens, slot, 1, 0)
        below = lax.ppermute(own_key, "group", [(g, (g + 1) % groups) for g in range(groups)])
        above = lax.ppermute(own_key, "group", [((g + 1) % groups, g) for g in range(groups)])
        return below, above

    normed = layer_norm(tokens).astype(jnp.bfloat16)
    queries = (
        jnp.dot(
            normed.reshape(views_here * length, features),
            w_query,
            preferred_element_type=jnp.float32,
        )
        .astype(jnp.bfloat16)
        .reshape(views_here, length, features)
    )
    is_key = (jnp.arange(views_here, dtype=jnp.int32) == slot_key).astype(jnp.int32)
    inverse = 1.0 / (counts + 2 * is_key).astype(jnp.float32)
    finish = (inverse, tokens, w_out)

    def make_table(phases, spots, key_phase, key_spot):
        key_rows = jnp.array([key_spot, key_spot + 1], jnp.int32)
        return jnp.stack(
            (
                jnp.concatenate((jnp.where(live, phases, 0), jnp.full((2,), key_phase, jnp.int32))),
                jnp.concatenate((spots, key_rows)),
                jnp.concatenate((entry_views, jnp.full((2,), 1, jnp.int32) * slot_key)),
            )
        )

    if not gather:
        cells = peers * capacity + ranks
        requests = (
            jnp.zeros((members * capacity,), jnp.int32)
            .at[cells]
            .set(places)
            .reshape(members, capacity)
        )
        asked = lax.all_to_all(requests, "member", split_axis=0, concat_axis=0, tiled=True)
        outgoing = tokens[asked.reshape(-1)].reshape(members, capacity, length, features)
        arrived = lax.all_to_all(outgoing, "member", split_axis=0, concat_axis=0, tiled=True)
        arrived = arrived.reshape(members * capacity, length, features)
        table = make_table(jnp.ones_like(cells), cells, 1, members * capacity)
        below, above = keyframes()
        blocks = [
            (0, arrived),
            (members * capacity, below),
            (members * capacity + 1, above),
        ]
        return add_phase(1, table, queries, w_key, w_value, blocks, None, finish)

    rows = members // ROW
    my_row, my_side = me // ROW, me % ROW
    peer_rows, peer_sides = peers // ROW, peers % ROW
    across = [(m, m ^ 1) for m in range(members)]

    def shift(block, step, up):
        route = []
        for m in range(members):
            row = m // ROW
            if up and row >= step - 1 and row + 1 < rows:
                route.append((m, m + ROW))
            if not up and row <= rows - step and row >= 1:
                route.append((m, m - ROW))
        return lax.ppermute(block, "member", route)

    def swap(block, step, up):
        route = [
            (m, other)
            for m, other in across
            if (m // ROW >= step if up else m // ROW <= rows - 1 - step)
        ]
        return lax.ppermute(block, "member", route)

    wanted = (
        (peer_rows[None, None, :] == jnp.arange(rows)[:, None, None])
        & (ranks[None, None, :] == jnp.arange(capacity)[None, :, None])
        & (peer_sides != my_side)[None, None, :]
    )
    request = jnp.sum(jnp.where(wanted, places[None, None, :], 0), axis=2)
    asked = lax.ppermute(request, "member", across)

    distance = jnp.abs(peer_rows - my_row)
    beside = peer_sides != my_side
    is_down = (peer_rows > my_row).astype(jnp.int32)
    phases = distance + beside.astype(jnp.int32)
    spots = jnp.where(
        beside,
        2 * views_here + jnp.where(distance == 0, places, is_down * capacity + ranks),
        is_down * views_here + places,
    )
    below, above = keyframes(asked)
    key_spot = 2 * views_here + 2 * capacity
    table = make_table(phases, spots, 2, key_spot)

    ups, downs = [tokens], [tokens]
    side_block = lax.ppermute(tokens, "member", across)
    for step in range(1, rows):
        ups.append(shift(ups[-1], step, True))
        downs.append(shift(downs[-1], step, False))
    total = None
    for phase in range(1, rows + 1):
        blocks = []
        if phase < rows:
            blocks += [(0, ups[phase]), (views_here, downs[phase])]
        if phase == 1:
            blocks.append((2 * views_here, side_block))
        else:
            step = phase - 1
            asked_up = lax.dynamic_index_in_dim(
                asked, jnp.maximum(my_row - step, 0), 0, keepdims=False
            )
            asked_down = lax.dynamic_index_in_dim(
                asked, jnp.minimum(my_row + step, rows - 1), 0, keepdims=False
            )
            blocks += [
                (2 * views_here, swap(pick(ups[step], asked_up), step, True)),
                (2 * views_here + capacity, swap(pick(downs[step], asked_down), step, False)),
            ]
        if phase == 2:
            blocks += [(key_spot, below), (key_spot + 1, above)]
        total = add_phase(
            phase,
            table,
            queries,
            w_key,
            w_value,
            blocks,
            total,
            finish if phase == rows else None,
        )
    return total


def solution(mesh):
    return jax.shard_map(
        sublayer,
        mesh=mesh,
        in_specs=(
            P(("group", "member"), None, None),
            P(),
            P(),
            P(),
            P(),
            P(("group", "member"), None),
            P(("group", "member")),
            P(("group", "member")),
        ),
        out_specs=P(("group", "member"), None, None),
        check_vma=False,
    )
```

profile of v0, /device:TPU:18, one launch (start us, length us, event | category | flops | bytes accessed | tf_op | source)
XLA Modules:
  0.0 189.7 jit_solution(15997549003734762715)
XLA Ops:
  0.0 3.6 %collective-permute-start.1 = (bf16[4,196,768]{2,0,1:T(4,128)(2,1)}, bf16[4,196,768]{2,0,1:T(4,128)(2,1)}, u32[]{:S(2)}, u32[]{:S(2)}) collective-permute-start(bf16[4,196,768]{2,0,1:T(4,128)(2,1)} %param.9), channel_id=1, source_target_pairs={{0,2},{1,3},{2,4},{3,5},{4,6},{5,7},{8,10},{9,11},{10,12},{11,13},... | collective-permute-start | bytes 3612680 | tf_op jit(solution)/shard_map/ppermute | solution.py:240
  3.6 2.4 %collective-permute-start.5 = (bf16[4,196,768]{2,0,1:T(4,128)(2,1)}, bf16[4,196,768]{2,0,1:T(4,128)(2,1)}, u32[]{:S(2)}, u32[]{:S(2)}) collective-permute-start(bf16[4,196,768]{2,0,1:T(4,128)(2,1)} %param.9), channel_id=1, source_target_pairs={{2,0},{3,1},{4,2},{5,3},{6,4},{7,5},{10,8},{11,9},{12,10},{13,11},... | collective-permute-start | bytes 3612680 | tf_op jit(solution)/shard_map/ppermute | solution.py:240
  8.4 22.2 %collective-permute-done.1 = bf16[4,196,768]{2,0,1:T(4,128)(2,1)} collective-permute-done((bf16[4,196,768]{2,0,1:T(4,128)(2,1)}, bf16[4,196,768]{2,0,1:T(4,128)(2,1)}, u32[]{:S(2)}, u32[]{:S(2)}) %collective-permute-start.1) | collective-permute-done | bytes 1204256 | tf_op jit(solution)/shard_map/ppermute | solution.py:240
  30.6 3.5 %collective-permute-start.2 = (bf16[4,196,768]{2,0,1:T(4,128)(2,1)}, bf16[4,196,768]{2,0,1:T(4,128)(2,1)}, u32[]{:S(2)}, u32[]{:S(2)}) collective-permute-start(bf16[4,196,768]{2,0,1:T(4,128)(2,1)} %collective-permute-done.1), channel_id=1, source_target_pairs={{2,4},{3,5},{4,6},{5,7},{10,12},{11,13},{12,14},{13,15},{18,20},{1... | collective-permute-start | bytes 3612680 | tf_op jit(solution)/shard_map/ppermute | solution.py:240
  34.1 4.5 %collective-permute-start.6 = (bf16[4,196,768]{2,0,1:T(4,128)(2,1)}, bf16[4,196,768]{2,0,1:T(4,128)(2,1)}, u32[]{:S(2)}, u32[]{:S(2)}) collective-permute-start(bf16[4,196,768]{2,0,1:T(4,128)(2,1)} %collective-permute-done.5), channel_id=1, source_target_pairs={{2,0},{3,1},{4,2},{5,3},{10,8},{11,9},{12,10},{13,11},{18,16},{19,... | collective-permute-start | bytes 3612680 | tf_op jit(solution)/shard_map/ppermute | solution.py:240
  39.4 2.5 %copy.50.refs_8_ = bf16[4,196,768]{2,1,0:T(8,128)(2,1)} copy(bf16[4,196,768]{2,0,1:T(4,128)(2,1)} %param.9) | data formatting | bytes 2408448 | tf_op args[0]
  44.3 15.9 %collective-permute-done.2 = bf16[4,196,768]{2,0,1:T(4,128)(2,1)} collective-permute-done((bf16[4,196,768]{2,0,1:T(4,128)(2,1)}, bf16[4,196,768]{2,0,1:T(4,128)(2,1)}, u32[]{:S(2)}, u32[]{:S(2)}) %collective-permute-start.2) | collective-permute-done | bytes 1204256 | tf_op jit(solution)/shard_map/ppermute | solution.py:240
  60.1 4.5 %collective-permute-start.3 = (bf16[4,196,768]{2,0,1:T(4,128)(2,1)}, bf16[4,196,768]{2,0,1:T(4,128)(2,1)}, u32[]{:S(2)}, u32[]{:S(2)}) collective-permute-start(bf16[4,196,768]{2,0,1:T(4,128)(2,1)} %collective-permute-done.2), channel_id=1, source_target_pairs={{4,6},{5,7},{12,14},{13,15},{20,22},{21,23},{28,30},{29,31}} | collective-permute-start | bytes 3612680 | tf_op jit(solution)/shard_map/ppermute | solution.py:240
  64.7 1.7 collective-permute-start.7
  70.0 2.4 %copy.57.source.refs_4_ = bf16[4,196,768]{2,1,0:T(8,128)(2,1)} copy(bf16[4,196,768]{2,0,1:T(4,128)(2,1)} %collective-permute-done.1) | data formatting | bytes 2408448 | tf_op jit(solution)/shard_map/ppermute | solution.py:240
  72.5 3.6 %pick_views.10 = bf16[3,196,768]{2,1,0:T(8,128)(2,1)} custom-call(s32[3]{0:T(128)} %get-tuple-element.8.index_ref, bf16[4,196,768]{2,1,0:T(8,128)(2,1)} %copy.57.source.refs_4_), custom_call_target="tpu_custom_call" | custom-call | tf_op jit(solution)/shard_map/pick_views/pallas_call | solution.py:142
  76.1 1.9 %collective-permute-start.11 = (bf16[3,196,768]{2,1,0:T(8,128)(2,1)}, bf16[3,196,768]{2,1,0:T(8,128)(2,1)}, u32[]{:S(2)}, u32[]{:S(2)}) collective-permute-start(bf16[3,196,768]{2,1,0:T(8,128)(2,1)} %pick_views.10), channel_id=1, source_target_pairs={{2,3},{3,2},{4,5},{5,4},{6,7},{7,6},{10,11},{11,10},{12,13},{13,12... | collective-permute-start | bytes 2709512 | tf_op jit(solution)/shard_map/ppermute | solution.py:248
  78.0 2.1 %convolution_convert_fusion = bf16[784,768]{1,0:T(8,128)(2,1)} fusion(bf16[784,768]{1,0:T(8,128)(2,1)S(1)} %reshape.248, bf16[768,768]{1,0:T(8,128)(2,1)S(1)} %copy-done), kind=kOutput, calls=%fused_computation.6 | convolution fusion | flops 925446144 | bytes 3588096 | tf_op jit(solution)/shard_map/dot_general | solution.py:184
  80.2 2.3 %reshape.249.refs_1_ = bf16[4,196,768]{2,1,0:T(8,128)(2,1)} reshape(bf16[784,768]{1,0:T(8,128)(2,1)} %convolution_convert_fusion) | data formatting | bytes 2408448 | tf_op jit(solution)/shard_map/reshape | solution.py:190
  82.4 2.5 %copy.58.source.refs_5_ = bf16[4,196,768]{2,1,0:T(8,128)(2,1)} copy(bf16[4,196,768]{2,0,1:T(4,128)(2,1)} %collective-permute-done.5) | data formatting | bytes 2408448 | tf_op jit(solution)/shard_map/ppermute | solution.py:240
  84.9 3.8 %pick_views.11 = bf16[3,196,768]{2,1,0:T(8,128)(2,1)} custom-call(s32[3]{0:T(128)} %get-tuple-element.7.index_ref, bf16[4,196,768]{2,1,0:T(8,128)(2,1)} %copy.58.source.refs_5_), custom_call_target="tpu_custom_call" | custom-call | tf_op jit(solution)/shard_map/pick_views/pallas_call | solution.py:142
  88.7 3.9 %collective-permute-start.12 = (bf16[3,196,768]{2,1,0:T(8,128)(2,1)}, bf16[3,196,768]{2,1,0:T(8,128)(2,1)}, u32[]{:S(2)}, u32[]{:S(2)}) collective-permute-start(bf16[3,196,768]{2,1,0:T(8,128)(2,1)} %pick_views.11), channel_id=1, source_target_pairs={{0,1},{1,0},{2,3},{3,2},{4,5},{5,4},{8,9},{9,8},{10,11},{11,10},{1... | collective-permute-start | bytes 2709512 | tf_op jit(solution)/shard_map/ppermute | solution.py:248
  93.3 2.5 %copy.56.source.refs_5_ = bf16[4,196,768]{2,1,0:T(8,128)(2,1)} copy(bf16[4,196,768]{2,0,1:T(4,128)(2,1)} %collective-permute-done.6) | data formatting | bytes 2408448 | tf_op jit(solution)/shard_map/ppermute | solution.py:240
  95.7 3.6 %pick_views.9 = bf16[3,196,768]{2,1,0:T(8,128)(2,1)} custom-call(s32[3]{0:T(128)} %get-tuple-element.9.index_ref, bf16[4,196,768]{2,1,0:T(8,128)(2,1)} %copy.56.source.refs_5_), custom_call_target="tpu_custom_call" | custom-call | tf_op jit(solution)/shard_map/pick_views/pallas_call | solution.py:142
  99.4 2.5 %copy.55.source.refs_4_ = bf16[4,196,768]{2,1,0:T(8,128)(2,1)} copy(bf16[4,196,768]{2,0,1:T(4,128)(2,1)} %collective-permute-done.2) | data formatting | bytes 2408448 | tf_op jit(solution)/shard_map/ppermute | solution.py:240
  101.9 3.8 %pick_views.8 = bf16[3,196,768]{2,1,0:T(8,128)(2,1)} custom-call(s32[3]{0:T(128)} %get-tuple-element.10.index_ref, bf16[4,196,768]{2,1,0:T(8,128)(2,1)} %copy.55.source.refs_4_), custom_call_target="tpu_custom_call" | custom-call | tf_op jit(solution)/shard_map/pick_views/pallas_call | solution.py:142
  107.3 1.9 %collective-permute-start.9 = (bf16[3,196,768]{2,1,0:T(8,128)(2,1)}, bf16[3,196,768]{2,1,0:T(8,128)(2,1)}, u32[]{:S(2)}, u32[]{:S(2)}) collective-permute-start(bf16[3,196,768]{2,1,0:T(8,128)(2,1)} %pick_views.8), channel_id=1, source_target_pairs={{4,5},{5,4},{6,7},{7,6},{12,13},{13,12},{14,15},{15,14},{20,21},{2... | collective-permute-start | bytes 2709512 | tf_op jit(solution)/shard_map/ppermute | solution.py:248
  109.8 2.5 %copy.62.refs_6_ = bf16[4,196,768]{2,1,0:T(8,128)(2,1)} copy(bf16[4,196,768]{2,0,1:T(4,128)(2,1)} %collective-permute-done.15) | data formatting | bytes 2408448 | tf_op jit(solution)/shard_map/ppermute | solution.py:272
  112.3 2.5 %copy.52.source.refs_4_ = bf16[4,196,768]{2,1,0:T(8,128)(2,1)} copy(bf16[4,196,768]{2,0,1:T(4,128)(2,1)} %collective-permute-done.3) | data formatting | bytes 2408448 | tf_op jit(solution)/shard_map/ppermute | solution.py:240
  114.8 3.6 %pick_views.6 = bf16[3,196,768]{2,1,0:T(8,128)(2,1)} custom-call(s32[3]{0:T(128)} %get-tuple-element.12.index_ref, bf16[4,196,768]{2,1,0:T(8,128)(2,1)} %copy.52.source.refs_4_), custom_call_target="tpu_custom_call" | custom-call | tf_op jit(solution)/shard_map/pick_views/pallas_call | solution.py:142
  118.4 2.4 %copy.54.source.refs_5_ = bf16[4,196,768]{2,1,0:T(8,128)(2,1)} copy(bf16[4,196,768]{2,0,1:T(4,128)(2,1)} %collective-permute-done.7) | data formatting | bytes 2408448 | tf_op jit(solution)/shard_map/ppermute | solution.py:240
  120.9 3.8 %pick_views.7 = bf16[3,196,768]{2,1,0:T(8,128)(2,1)} custom-call(s32[3]{0:T(128)} %get-tuple-element.11.index_ref, bf16[4,196,768]{2,1,0:T(8,128)(2,1)} %copy.54.source.refs_5_), custom_call_target="tpu_custom_call" | custom-call | tf_op jit(solution)/shard_map/pick_views/pallas_call | solution.py:142
  126.3 16.4 %attend_phase.4.refs_10_ = f32[4,196,768]{2,1,0:T(8,128)} custom-call(s32[3,18]{1,0:T(4,128)} %pad_add_fusion.refs_0_, bf16[4,196,768]{2,1,0:T(8,128)(2,1)} %reshape.249.refs_1_, bf16[768,768]{1,0:T(8,128)(2,1)} %refs_2_.7, bf16[768,768]{1,0:T(8,128)(2,1)} %refs_3_.7, bf16[4,196,768]{2,1,0:T(8,128)(2,1)} %copy.57.source.refs_4_, ...), custom_call_target="tpu_custom_call" | custom-call | flops 3737911296 | bytes 4816896 | tf_op jit(solution)/shard_map/attend_phase/pallas_call | solution.py:114
  142.6 23.0 %attend_phase.5.refs_8_ = f32[4,196,768]{2,1,0:T(8,128)} custom-call(s32[3,18]{1,0:T(4,128)} %pad_add_fusion.refs_0_, bf16[4,196,768]{2,1,0:T(8,128)(2,1)} %reshape.249.refs_1_, bf16[768,768]{1,0:T(8,128)(2,1)} %refs_2_.7, bf16[768,768]{1,0:T(8,128)(2,1)} %refs_3_.7, bf16[4,196,768]{2,1,0:T(8,128)(2,1)} %copy.55.source.refs_4_, ...), custom_call_target="tpu_custom_call" | custom-call | flops 3737911296 | bytes 4816896 | tf_op jit(solution)/shard_map/attend_phase/pallas_call | solution.py:114
  165.7 12.1 %attend_phase.6.refs_6_ = f32[4,196,768]{2,1,0:T(8,128)} custom-call(s32[3,18]{1,0:T(4,128)} %pad_add_fusion.refs_0_, bf16[4,196,768]{2,1,0:T(8,128)(2,1)} %reshape.249.refs_1_, bf16[768,768]{1,0:T(8,128)(2,1)} %refs_2_.7, bf16[768,768]{1,0:T(8,128)(2,1)} %refs_3_.7, bf16[4,196,768]{2,1,0:T(8,128)(2,1)} %copy.52.source.refs_4_, ...), custom_call_target="tpu_custom_call" | custom-call | flops 3737911296 | bytes 4816896 | tf_op jit(solution)/shard_map/attend_phase/pallas_call | solution.py:114
  179.7 7.2 %attend_phase.7 = bf16[4,196,768]{2,1,0:T(8,128)(2,1)} custom-call(s32[3,18]{1,0:T(4,128)} %pad_add_fusion.refs_0_, bf16[4,196,768]{2,1,0:T(8,128)(2,1)} %reshape.249.refs_1_, bf16[768,768]{1,0:T(8,128)(2,1)} %refs_2_.7, bf16[768,768]{1,0:T(8,128)(2,1)} %refs_3_.7, bf16[3,196,768]{2,1,0:T(8,128)(2,1)} %copy-done.4, bf16[3,196,768]{2,1,0:T(8,128)(2,1)} %copy-done.5, ...), custom_call_target="tpu_custom_call" | custom-call | flops 3737911296 | bytes 4816896 | tf_op jit(solution)/shard_map/attend_phase/pallas_call | solution.py:114
  186.9 2.8 %copy.67 = bf16[4,196,768]{2,0,1:T(4,128)(2,1)} copy(bf16[4,196,768]{2,1,0:T(8,128)(2,1)} %attend_phase.7) | data formatting | bytes 2408448 | tf_op jit(solution)/shard_map/attend_phase/pallas_call | solution.py:114
  (61 shorter events, 15.0 us)
Async XLA Ops:
  0.0 78.0 %copy-start = (bf16[768,768]{1,0:T(8,128)(2,1)S(1)}, bf16[768,768]{1,0:T(8,128)(2,1)}, u32[]{:S(2)}) copy-start(bf16[768,768]{1,0:T(8,128)(2,1)} %param.10) | copy-start | bytes 3538948
  0.0 30.6 %collective-permute-start.1 = (bf16[4,196,768]{2,0,1:T(4,128)(2,1)}, bf16[4,196,768]{2,0,1:T(4,128)(2,1)}, u32[]{:S(2)}, u32[]{:S(2)}) collective-permute-start(bf16[4,196,768]{2,0,1:T(4,128)(2,1)} %param.9), channel_id=1, source_target_pairs={{0,2},{1,3},{2,4},{3,5},{4,6},{5,7},{8,10},{9,11},{10,12},{11,13},... | collective-permute-start | bytes 3612680 | tf_op jit(solution)/shard_map/ppermute | solution.py:240
  3.6 30.4 %collective-permute-start.5 = (bf16[4,196,768]{2,0,1:T(4,128)(2,1)}, bf16[4,196,768]{2,0,1:T(4,128)(2,1)}, u32[]{:S(2)}, u32[]{:S(2)}) collective-permute-start(bf16[4,196,768]{2,0,1:T(4,128)(2,1)} %param.9), channel_id=1, source_target_pairs={{2,0},{3,1},{4,2},{5,3},{6,4},{7,5},{10,8},{11,9},{12,10},{13,11},... | collective-permute-start | bytes 3612680 | tf_op jit(solution)/shard_map/ppermute | solution.py:240
  6.0 86.7 %collective-permute-start.15 = (bf16[4,196,768]{2,0,1:T(4,128)(2,1)}, bf16[4,196,768]{2,0,1:T(4,128)(2,1)}, u32[]{:S(2)}, u32[]{:S(2)}) collective-permute-start(bf16[4,196,768]{2,0,1:T(4,128)(2,1)} %param.9), channel_id=1, source_target_pairs={{0,1},{1,0},{2,3},{3,2},{4,5},{5,4},{6,7},{7,6},{8,9},{9,8},{10,11... | collective-permute-start | bytes 3612680 | tf_op jit(solution)/shard_map/ppermute | solution.py:272
  30.6 29.6 %collective-permute-start.2 = (bf16[4,196,768]{2,0,1:T(4,128)(2,1)}, bf16[4,196,768]{2,0,1:T(4,128)(2,1)}, u32[]{:S(2)}, u32[]{:S(2)}) collective-permute-start(bf16[4,196,768]{2,0,1:T(4,128)(2,1)} %collective-permute-done.1), channel_id=1, source_target_pairs={{2,4},{3,5},{4,6},{5,7},{10,12},{11,13},{12,14},{13,15},{18,20},{1... | collective-permute-start | bytes 3612680 | tf_op jit(solution)/shard_map/ppermute | solution.py:240
  34.1 30.6 %collective-permute-start.6 = (bf16[4,196,768]{2,0,1:T(4,128)(2,1)}, bf16[4,196,768]{2,0,1:T(4,128)(2,1)}, u32[]{:S(2)}, u32[]{:S(2)}) collective-permute-start(bf16[4,196,768]{2,0,1:T(4,128)(2,1)} %collective-permute-done.5), channel_id=1, source_target_pairs={{2,0},{3,1},{4,2},{5,3},{10,8},{11,9},{12,10},{13,11},{18,16},{19,... | collective-permute-start | bytes 3612680 | tf_op jit(solution)/shard_map/ppermute | solution.py:240
  38.7 4.8 %copy-start.1 = (bf16[4,196,768]{2,0,1:T(4,128)(2,1)S(1)}, bf16[4,196,768]{2,0,1:T(4,128)(2,1)}, u32[]{:S(2)}) copy-start(bf16[4,196,768]{2,0,1:T(4,128)(2,1)} %param.9) | copy-start | bytes 3612676
  38.8 30.4 %collective-permute-start = (s32[4,3]{0,1:T(4,128)S(1)}, s32[4,3]{0,1:T(4,128)S(1)}, u32[]{:S(2)}, u32[]{:S(2)}) collective-permute-start(s32[4,3]{0,1:T(4,128)S(1)} %select_reduce_fusion), channel_id=1, source_target_pairs={{0,1},{1,0},{2,3},{3,2},{4,5},{5,4},{6,7},{7,6},{8,9},{9,8},{10,11... | collective-permute-start | bytes 152 | tf_op jit(solution)/shard_map/ppermute | solution.py:256
  43.5 45.2 %collective-permute-start.13 = (bf16[1,196,768]{2,1,0:T(8,128)(2,1)S(1)}, bf16[1,196,768]{2,1,0:T(8,128)(2,1)S(1)}, u32[]{:S(2)}, u32[]{:S(2)}) collective-permute-start(bf16[1,196,768]{2,1,0:T(8,128)(2,1)S(1)} %constant_dynamic-slice_fusion), channel_id=1, source_target_pairs={{0,8},{8,16},{16,24},{24,0},{1,9},{9,17},{17,25},{25,1},{2,10},{10... | collective-permute-start | bytes 903176 | tf_op jit(solution)/shard_map/ppermute | solution.py:178
  60.1 45.5 %collective-permute-start.3 = (bf16[4,196,768]{2,0,1:T(4,128)(2,1)}, bf16[4,196,768]{2,0,1:T(4,128)(2,1)}, u32[]{:S(2)}, u32[]{:S(2)}) collective-permute-start(bf16[4,196,768]{2,0,1:T(4,128)(2,1)} %collective-permute-done.2), channel_id=1, source_target_pairs={{4,6},{5,7},{12,14},{13,15},{20,22},{21,23},{28,30},{29,31}} | collective-permute-start | bytes 3612680 | tf_op jit(solution)/shard_map/ppermute | solution.py:240
  64.7 42.6 %collective-permute-start.7 = (bf16[4,196,768]{2,0,1:T(4,128)(2,1)}, bf16[4,196,768]{2,0,1:T(4,128)(2,1)}, u32[]{:S(2)}, u32[]{:S(2)}) collective-permute-start(bf16[4,196,768]{2,0,1:T(4,128)(2,1)} %collective-permute-done.6), channel_id=1, source_target_pairs={{2,0},{3,1},{10,8},{11,9},{18,16},{19,17},{26,24},{27,25}} | collective-permute-start | bytes 3612680 | tf_op jit(solution)/shard_map/ppermute | solution.py:240
  76.1 49.2 %collective-permute-start.11 = (bf16[3,196,768]{2,1,0:T(8,128)(2,1)}, bf16[3,196,768]{2,1,0:T(8,128)(2,1)}, u32[]{:S(2)}, u32[]{:S(2)}) collective-permute-start(bf16[3,196,768]{2,1,0:T(8,128)(2,1)} %pick_views.10), channel_id=1, source_target_pairs={{2,3},{3,2},{4,5},{5,4},{6,7},{7,6},{10,11},{11,10},{12,13},{13,12... | collective-permute-start | bytes 2709512 | tf_op jit(solution)/shard_map/ppermute | solution.py:248
  84.9 7.7 %copy-start.8 = (s32[2]{0:T(128)S(1)}, s32[2]{0:T(128)}, u32[]{:S(2)}) copy-start(s32[2]{0:T(128)} %constant.140.clone) | copy-start | bytes 28
  88.7 10.7 %copy-start.6 = (bf16[1,196,768]{2,1,0:T(8,128)(2,1)}, bf16[1,196,768]{2,1,0:T(8,128)(2,1)S(1)}, u32[]{:S(2)}) copy-start(bf16[1,196,768]{2,1,0:T(8,128)(2,1)S(1)} %collective-permute-done.13.refs_8_) | copy-start | bytes 903172
  88.7 54.0 %collective-permute-start.12 = (bf16[3,196,768]{2,1,0:T(8,128)(2,1)}, bf16[3,196,768]{2,1,0:T(8,128)(2,1)}, u32[]{:S(2)}, u32[]{:S(2)}) collective-permute-start(bf16[3,196,768]{2,1,0:T(8,128)(2,1)} %pick_views.11), channel_id=1, source_target_pairs={{0,1},{1,0},{2,3},{3,2},{4,5},{5,4},{8,9},{9,8},{10,11},{11,10},{1... | collective-permute-start | bytes 2709512 | tf_op jit(solution)/shard_map/ppermute | solution.py:248
  92.7 32.0 %collective-permute-start.14 = (bf16[1,196,768]{2,1,0:T(8,128)(2,1)S(1)}, bf16[1,196,768]{2,1,0:T(8,128)(2,1)}, u32[]{:S(2)}, u32[]{:S(2)}) collective-permute-start(bf16[1,196,768]{2,1,0:T(8,128)(2,1)S(1)} %constant_dynamic-slice_fusion), channel_id=1, source_target_pairs={{8,0},{16,8},{24,16},{0,24},{9,1},{17,9},{25,17},{1,25},{10,2},{18... | collective-permute-start | bytes 903176 | tf_op jit(solution)/shard_map/ppermute | solution.py:179
  101.9 3.8 %copy-start.2 = (bf16[3,196,768]{2,1,0:T(8,128)(2,1)S(1)}, bf16[3,196,768]{2,1,0:T(8,128)(2,1)}, u32[]{:S(2)}) copy-start(bf16[3,196,768]{2,1,0:T(8,128)(2,1)} %pick_views.9) | copy-start | bytes 2709508
  101.9 7.3 %copy-start.7 = (s32[4]{0:T(128)S(1)}, s32[4]{0:T(128)}, u32[]{:S(2)}) copy-start(s32[4]{0:T(128)} %param.15) | copy-start | bytes 52
  105.7 60.0 %collective-permute-start.10 = (bf16[3,196,768]{2,1,0:T(8,128)(2,1)S(1)}, bf16[3,196,768]{2,1,0:T(8,128)(2,1)}, u32[]{:S(2)}, u32[]{:S(2)}) collective-permute-start(bf16[3,196,768]{2,1,0:T(8,128)(2,1)S(1)} %copy-done.2), channel_id=1, source_target_pairs={{0,1},{1,0},{2,3},{3,2},{8,9},{9,8},{10,11},{11,10},{16,17},{17,16... | collective-permute-start | bytes 2709512 | tf_op jit(solution)/shard_map/ppermute | solution.py:248
  107.3 58.4 %collective-permute-start.9 = (bf16[3,196,768]{2,1,0:T(8,128)(2,1)}, bf16[3,196,768]{2,1,0:T(8,128)(2,1)}, u32[]{:S(2)}, u32[]{:S(2)}) collective-permute-start(bf16[3,196,768]{2,1,0:T(8,128)(2,1)} %pick_views.8), channel_id=1, source_target_pairs={{4,5},{5,4},{6,7},{7,6},{12,13},{13,12},{14,15},{15,14},{20,21},{2... | collective-permute-start | bytes 2709512 | tf_op jit(solution)/shard_map/ppermute | solution.py:248
  120.9 3.8 %copy-start.3 = (bf16[3,196,768]{2,1,0:T(8,128)(2,1)S(1)}, bf16[3,196,768]{2,1,0:T(8,128)(2,1)}, u32[]{:S(2)}) copy-start(bf16[3,196,768]{2,1,0:T(8,128)(2,1)} %pick_views.6) | copy-start | bytes 2709508
  124.6 53.1 %collective-permute-start.4 = (bf16[3,196,768]{2,1,0:T(8,128)(2,1)S(1)}, bf16[3,196,768]{2,1,0:T(8,128)(2,1)S(1)}, u32[]{:S(2)}, u32[]{:S(2)}) collective-permute-start(bf16[3,196,768]{2,1,0:T(8,128)(2,1)S(1)} %copy-done.3), channel_id=1, source_target_pairs={{6,7},{7,6},{14,15},{15,14},{22,23},{23,22},{30,31},{31,30}} | collective-permute-start | bytes 2709512 | tf_op jit(solution)/shard_map/ppermute | solution.py:248
  125.4 52.4 %collective-permute-start.8 = (bf16[3,196,768]{2,1,0:T(8,128)(2,1)}, bf16[3,196,768]{2,1,0:T(8,128)(2,1)S(1)}, u32[]{:S(2)}, u32[]{:S(2)}) collective-permute-start(bf16[3,196,768]{2,1,0:T(8,128)(2,1)} %pick_views.7), channel_id=1, source_target_pairs={{0,1},{1,0},{8,9},{9,8},{16,17},{17,16},{24,25},{25,24}} | collective-permute-start | bytes 2709512 | tf_op jit(solution)/shard_map/ppermute | solution.py:248
  177.8 0.9 copy-start.4
  178.7 1.0 copy-start.5
where the time goes:
time: 191 us; the launch traced here: 190 us
  Pallas kernels  80.8 us (42%)
  waiting for transfers between devices  38.1 us (20%)
  starting transfers between devices  32.4 us (17%)
  local copies, waits for them, and re-layouts  30.8 us (16%)
  other arithmetic  4.5 us (2%)
  matrix products  2.13 us (1%)
    pallas_call x4, Pallas kernels, add_phase(): pl.pallas_call(functools.partial(step_kernel, phase, first, final, places...  58.7 us
    ppermute x6, waiting for transfers between devices, shift(): return lax.ppermute(block, 'member', route)  38 us
    pallas_call x6, Pallas kernels, pick(): pl.pallas_call(copy_view, grid_spec=pltpu.PrefetchScalarGridSpec(num_scal...  22.2 us
    ppermute x6, starting transfers between devices, shift(): return lax.ppermute(block, 'member', route)  20.2 us
    ppermute x6, local copies, waits for them, and re-layouts, shift(): return lax.ppermute(block, 'member', route)  14.8 us
    ppermute x6, starting transfers between devices, swap(): return lax.ppermute(block, 'member', route)  11 us
    unnamed x19, local copies, waits for them, and re-layouts  4.39 us
  transfers between devices with their start and end apart: 16, of which 2 were waited for; matrix products, arithmetic and copies ran while one was open for 17% of the time, Pallas kernels for 39%

commit v1 on v0

--- a/solution.py
+++ b/solution.py
@@ -5,7 +5,6 @@
 from jax import lax
 from jax.experimental import pallas as pl
 from jax.experimental.pallas import tpu as pltpu
-from jax.experimental.layout import Layout, with_layout_constraint
 from jax.sharding import PartitionSpec as P
 
 
@@ -43,7 +42,7 @@
         total[...] = jnp.zeros_like(total)
     for copy in copies:
         copy.wait()
-    views, _, features = queries.shape
+    views, length, features = total.shape
     size = features // HEADS
     lanes = lax.broadcasted_iota(jnp.int32, (1, 2 * size), 1)
     lower = lanes < size
@@ -52,7 +51,7 @@
         @pl.when(table[0, e] == phase)
         def _():
             place, view = table[1, e], table[2, e]
-            normed = layer_norm(held[place]).astype(jnp.bfloat16)
+            normed = layer_norm(held[place, :length, :]).astype(jnp.bfloat16)
             pair[:, :features] = jnp.dot(
                 normed, w_key[...], preferred_element_type=jnp.float32
             ).astype(jnp.bfloat16)
@@ -61,7 +60,7 @@
             ).astype(jnp.bfloat16)
             for h in range(HEADS // 2):
                 cols = pl.ds(2 * h * size, 2 * size)
-                query = queries[view, :, cols] * jnp.bfloat16(size**-0.5)
+                query = queries[view, :length, cols] * jnp.bfloat16(size**-0.5)
                 key = pair[:, cols]
                 value = pair[:, pl.ds(features + 2 * h * size, 2 * size)]
                 halves = []
@@ -86,15 +85,15 @@
         for v in range(views):
             mixed = (total[v] * inverse[v]).astype(jnp.bfloat16)
             projected = jnp.dot(mixed, w_out[...], preferred_element_type=jnp.float32)
-            out_ref[v] = (tokens[v].astype(jnp.float32) + projected).astype(out_ref.dtype)
+            out_ref[v] = (tokens[v, :length, :].astype(jnp.float32) + projected).astype(out_ref.dtype)
     else:
         copy = pltpu.make_async_copy(total, out_ref, sems.at[0])
         copy.start()
         copy.wait()
 
 
-def add_phase(phase, table, queries, w_key, w_value, blocks, total, finish=None):
-    views, length, features = queries.shape
+def add_phase(length, phase, table, queries, w_key, w_value, blocks, total, finish=None):
+    views, padded, features = queries.shape
     first, final = total is None, finish is not None
     places = [place for place, _ in blocks]
     arrays = [block for _, block in blocks]
@@ -114,12 +113,12 @@
     return pl.pallas_call(
         functools.partial(step_kernel, phase, first, final, places),
         out_shape=jax.ShapeDtypeStruct(
-            queries.shape, jnp.bfloat16 if final else jnp.float32
+            (views, length, features), jnp.bfloat16 if final else jnp.float32
         ),
         in_specs=specs,
         out_specs=vmem if final else hbm,
         scratch_shapes=[
-            pltpu.VMEM((depth, length, features), jnp.bfloat16),
+            pltpu.VMEM((depth, padded, features), jnp.bfloat16),
             pltpu.VMEM((length, 2 * features), jnp.bfloat16),
             pltpu.VMEM((views, length, features), jnp.float32),
             pltpu.SemaphoreType.DMA((len(arrays) + 1,)),
@@ -135,26 +134,33 @@
 
 
 def pick(block, indices):
-    def copy_view(index_ref, source, target):
-        target[...] = source[...]
-
-    shape = (1,) + block.shape[1:]
+    def copy_views(index, source, target, sems):
+        copies = [
+            pltpu.make_async_copy(source.at[index[i]], target.at[i], sems.at[i])
+            for i in range(target.shape[0])
+        ]
+        for copy in copies:
+            copy.start()
+        for copy in copies:
+            copy.wait()
+
     return pl.pallas_call(
-        copy_view,
-        grid_spec=pltpu.PrefetchScalarGridSpec(
-            num_scalar_prefetch=1,
-            grid=indices.shape,
-            in_specs=[pl.BlockSpec(shape, lambda i, index: (index[i], 0, 0))],
-            out_specs=pl.BlockSpec(shape, lambda i, index: (i, 0, 0)),
-        ),
+        copy_views,
+        in_specs=[
+            pl.BlockSpec(memory_space=pltpu.SMEM),
+            pl.BlockSpec(memory_space=pl.ANY),
+        ],
+        out_specs=pl.BlockSpec(memory_space=pltpu.VMEM),
         out_shape=jax.ShapeDtypeStruct(indices.shape + block.shape[1:], block.dtype),
+        scratch_shapes=[pltpu.SemaphoreType.DMA(indices.shape)],
         name="pick_views",
     )(indices, block)
 
 
 def sublayer(tokens, w_query, w_key, w_value, w_out, partners, counts, key_slot):
     views_here, length, features = tokens.shape
-    tokens = with_layout_constraint(tokens, Layout(major_to_minor=(0, 1, 2)))
+    tokens = jnp.pad(tokens, ((0, 0), (0, -length % 8), (0, 0)))
+    padded = tokens.shape[1]
     members = lax.axis_size("member")
     groups = lax.axis_size("group")
     me = lax.axis_index("member")
@@ -180,15 +186,12 @@
         return below, above
 
     normed = layer_norm(tokens).astype(jnp.bfloat16)
-    queries = (
-        jnp.dot(
-            normed.reshape(views_here * length, features),
-            w_query,
-            preferred_element_type=jnp.float32,
-        )
-        .astype(jnp.bfloat16)
-        .reshape(views_here, length, features)
-    )
+    queries = jnp.dot(
+        normed.reshape(views_here * padded, features),
+        w_query,
+        preferred_element_type=jnp.float32,
+    ).astype(jnp.bfloat16)
+    queries = queries.reshape(views_here, padded, features)
     is_key = (jnp.arange(views_here, dtype=jnp.int32) == slot_key).astype(jnp.int32)
     inverse = 1.0 / (counts + 2 * is_key).astype(jnp.float32)
     finish = (inverse, tokens, w_out)
@@ -212,9 +215,9 @@
             .reshape(members, capacity)
         )
         asked = lax.all_to_all(requests, "member", split_axis=0, concat_axis=0, tiled=True)
-        outgoing = tokens[asked.reshape(-1)].reshape(members, capacity, length, features)
+        outgoing = tokens[asked.reshape(-1)].reshape(members, capacity, padded, features)
         arrived = lax.all_to_all(outgoing, "member", split_axis=0, concat_axis=0, tiled=True)
-        arrived = arrived.reshape(members * capacity, length, features)
+        arrived = arrived.reshape(members * capacity, padded, features)
         table = make_table(jnp.ones_like(cells), cells, 1, members * capacity)
         below, above = keyframes()
         blocks = [
@@ -222,7 +225,7 @@
             (members * capacity, below),
             (members * capacity + 1, above),
         ]
-        return add_phase(1, table, queries, w_key, w_value, blocks, None, finish)
+        return add_phase(length, 1, table, queries, w_key, w_value, blocks, None, finish)
 
     rows = members // ROW
     my_row, my_side = me // ROW, me % ROW
@@ -295,6 +298,7 @@
         if phase == 2:
             blocks += [(key_spot, below), (key_spot + 1, above)]
         total = add_phase(
+            length,
             phase,
             table,
             queries,

time: 191 us -> 169 us (0.88)
  local copies, waits for them, and re-layouts: 30.8 us -> 8.36 us
  waiting for transfers between devices: 38.1 us -> 43.8 us
  Pallas kernels: 80.8 us -> 75.7 us
    ppermute x7 -> x0, local copies, waits for them, and re-layouts: 17.3 us -> none  [the longest x6 14.8 us: shift(): return lax.ppermute(block, 'member', route)]
    ppermute x6, waiting for transfers between devices: 38 us -> 43.8 us  [shift(): return lax.ppermute(block, 'member', route)]
    pallas_call x6, Pallas kernels: 22.2 us -> 17 us  [pick(): pl.pallas_call(copy_views, in_specs=[pl.BlockSpec(memory_space=pltpu.SMEM...]
    reshape x2 -> x0, local copies, waits for them, and re-layouts: 3.65 us -> none  [the longest x1 2.26 us: sublayer(): queries = jnp.dot(normed.reshape(views_here * length, features), w_query,...]
    unnamed x19 -> x23, local copies, waits for them, and re-layouts: 4.39 us -> 3.42 us
  transfers between devices with their start and end apart: 16 -> 16, of which waited for: 2 -> 2; matrix products, arithmetic and copies ran while one was open for 17% -> 4% of each run, Pallas kernels for 39% -> 41%
where the time goes in v1:
time: 169 us; the launch traced here: 168 us
  Pallas kernels  75.7 us (45%)
  waiting for transfers between devices  43.8 us (26%)
  starting transfers between devices  32.9 us (19%)
  local copies, waits for them, and re-layouts  8.36 us (5%)
  other arithmetic  3.85 us (2%)
  matrix products  2.16 us (1%)
    pallas_call x4, Pallas kernels, add_phase(): pl.pallas_call(functools.partial(step_kernel, phase, first, final, places...  58.6 us
    ppermute x6, waiting for transfers between devices, shift(): return lax.ppermute(block, 'member', route)  43.8 us
    ppermute x6, starting transfers between devices, shift(): return lax.ppermute(block, 'member', route)  20.1 us
    pallas_call x6, Pallas kernels, pick(): pl.pallas_call(copy_views, in_specs=[pl.BlockSpec(memory_space=pltpu.SMEM...  17 us
    ppermute x6, starting transfers between devices, swap(): return lax.ppermute(block, 'member', route)  11.5 us
    unnamed x23, local copies, waits for them, and re-layouts  3.42 us
  transfers between devices with their start and end apart: 16, of which 2 were waited for; matrix products, arithmetic and copies ran while one was open for 4% of the time, Pallas kernels for 41%

profile of v1, /device:TPU:18, one launch (start us, length us, event | category | flops | bytes accessed | tf_op | source)
XLA Modules:
  0.0 167.9 jit_solution(7552464311275868125)
XLA Ops:
  0.0 1.5 copy.14
  1.5 1.1 pad.6.refs_8_
  2.7 3.5 %collective-permute-start.1 = (bf16[4,200,768]{2,1,0:T(8,128)(2,1)}, bf16[4,200,768]{2,1,0:T(8,128)(2,1)}, u32[]{:S(2)}, u32[]{:S(2)}) collective-permute-start(bf16[4,200,768]{2,1,0:T(8,128)(2,1)} %pad.6.refs_8_), channel_id=1, source_target_pairs={{0,2},{1,3},{2,4},{3,5},{4,6},{5,7},{8,10},{9,11},{10,12},{11,13},... | collective-permute-start | bytes 3686408 | tf_op jit(solution)/shard_map/ppermute | solution.py:243
  6.2 2.4 %collective-permute-start.5 = (bf16[4,200,768]{2,1,0:T(8,128)(2,1)}, bf16[4,200,768]{2,1,0:T(8,128)(2,1)}, u32[]{:S(2)}, u32[]{:S(2)}) collective-permute-start(bf16[4,200,768]{2,1,0:T(8,128)(2,1)} %pad.6.refs_8_), channel_id=1, source_target_pairs={{2,0},{3,1},{4,2},{5,3},{6,4},{7,5},{10,8},{11,9},{12,10},{13,11},... | collective-permute-start | bytes 3686408 | tf_op jit(solution)/shard_map/ppermute | solution.py:243
  9.6 24.0 %collective-permute-done.1.source.refs_4_ = bf16[4,200,768]{2,1,0:T(8,128)(2,1)} collective-permute-done((bf16[4,200,768]{2,1,0:T(8,128)(2,1)}, bf16[4,200,768]{2,1,0:T(8,128)(2,1)}, u32[]{:S(2)}, u32[]{:S(2)}) %collective-permute-start.1) | collective-permute-done | bytes 1228832 | tf_op jit(solution)/shard_map/ppermute | solution.py:243
  33.6 3.5 %collective-permute-start.2 = (bf16[4,200,768]{2,1,0:T(8,128)(2,1)}, bf16[4,200,768]{2,1,0:T(8,128)(2,1)}, u32[]{:S(2)}, u32[]{:S(2)}) collective-permute-start(bf16[4,200,768]{2,1,0:T(8,128)(2,1)} %collective-permute-done.1.source.refs_4_), channel_id=1, source_target_pairs={{2,4},{3,5},{4,6},{5,7},{10,12},{11,13},{12,14},{13,15},{18,20},{1... | collective-permute-start | bytes 3686408 | tf_op jit(solution)/shard_map/ppermute | solution.py:243
  37.1 4.5 %collective-permute-start.6 = (bf16[4,200,768]{2,1,0:T(8,128)(2,1)}, bf16[4,200,768]{2,1,0:T(8,128)(2,1)}, u32[]{:S(2)}, u32[]{:S(2)}) collective-permute-start(bf16[4,200,768]{2,1,0:T(8,128)(2,1)} %collective-permute-done.5.source.refs_5_), channel_id=1, source_target_pairs={{2,0},{3,1},{4,2},{5,3},{10,8},{11,9},{12,10},{13,11},{18,16},{19,... | collective-permute-start | bytes 3686408 | tf_op jit(solution)/shard_map/ppermute | solution.py:243
  44.0 19.8 %collective-permute-done.2.source.refs_4_ = bf16[4,200,768]{2,1,0:T(8,128)(2,1)} collective-permute-done((bf16[4,200,768]{2,1,0:T(8,128)(2,1)}, bf16[4,200,768]{2,1,0:T(8,128)(2,1)}, u32[]{:S(2)}, u32[]{:S(2)}) %collective-permute-start.2) | collective-permute-done | bytes 1228832 | tf_op jit(solution)/shard_map/ppermute | solution.py:243
  63.7 4.5 %collective-permute-start.3 = (bf16[4,200,768]{2,1,0:T(8,128)(2,1)}, bf16[4,200,768]{2,1,0:T(8,128)(2,1)}, u32[]{:S(2)}, u32[]{:S(2)}) collective-permute-start(bf16[4,200,768]{2,1,0:T(8,128)(2,1)} %collective-permute-done.2.source.refs_4_), channel_id=1, source_target_pairs={{4,6},{5,7},{12,14},{13,15},{20,22},{21,23},{28,30},{29,31}} | collective-permute-start | bytes 3686408 | tf_op jit(solution)/shard_map/ppermute | solution.py:243
  68.3 1.7 %collective-permute-start.7 = (bf16[4,200,768]{2,1,0:T(8,128)(2,1)}, bf16[4,200,768]{2,1,0:T(8,128)(2,1)}, u32[]{:S(2)}, u32[]{:S(2)}) collective-permute-start(bf16[4,200,768]{2,1,0:T(8,128)(2,1)} %collective-permute-done.6.source.refs_5_), channel_id=1, source_target_pairs={{2,0},{3,1},{10,8},{11,9},{18,16},{19,17},{26,24},{27,25}} | collective-permute-start | bytes 3686408 | tf_op jit(solution)/shard_map/ppermute | solution.py:243
  70.1 0.8 dynamic-slice_reduce_fusion
  70.9 2.8 %pick_views.10 = bf16[3,200,768]{2,1,0:T(8,128)(2,1)} custom-call(s32[3]{0:T(128)} %get-tuple-element.8.index, bf16[4,200,768]{2,1,0:T(8,128)(2,1)} %collective-permute-done.1.source.refs_4_), custom_call_target="tpu_custom_call" | custom-call | tf_op jit(solution)/shard_map/pick_views/pallas_call | solution.py:147
  73.7 2.4 %collective-permute-start.11 = (bf16[3,200,768]{2,1,0:T(8,128)(2,1)}, bf16[3,200,768]{2,1,0:T(8,128)(2,1)}, u32[]{:S(2)}, u32[]{:S(2)}) collective-permute-start(bf16[3,200,768]{2,1,0:T(8,128)(2,1)} %pick_views.10), channel_id=1, source_target_pairs={{2,3},{3,2},{4,5},{5,4},{6,7},{7,6},{10,11},{11,10},{12,13},{13,12... | collective-permute-start | bytes 2764808 | tf_op jit(solution)/shard_map/ppermute | solution.py:251
  76.3 1.4 fusion.3
  77.7 2.9 %pick_views.11 = bf16[3,200,768]{2,1,0:T(8,128)(2,1)} custom-call(s32[3]{0:T(128)} %get-tuple-element.7.index, bf16[4,200,768]{2,1,0:T(8,128)(2,1)} %collective-permute-done.5.source.refs_5_), custom_call_target="tpu_custom_call" | custom-call | tf_op jit(solution)/shard_map/pick_views/pallas_call | solution.py:147
  80.6 3.4 %collective-permute-start.12 = (bf16[3,200,768]{2,1,0:T(8,128)(2,1)}, bf16[3,200,768]{2,1,0:T(8,128)(2,1)}, u32[]{:S(2)}, u32[]{:S(2)}) collective-permute-start(bf16[3,200,768]{2,1,0:T(8,128)(2,1)} %pick_views.11), channel_id=1, source_target_pairs={{0,1},{1,0},{2,3},{3,2},{4,5},{5,4},{8,9},{9,8},{10,11},{11,10},{1... | collective-permute-start | bytes 2764808 | tf_op jit(solution)/shard_map/ppermute | solution.py:251
  84.6 2.2 %convolution_convert_fusion = bf16[800,768]{1,0:T(8,128)(2,1)} fusion(bf16[800,768]{1,0:T(8,128)(2,1)S(1)} %bitcast.16, bf16[768,768]{1,0:T(8,128)(2,1)S(1)} %copy-done), kind=kOutput, calls=%fused_computation.6 | convolution fusion | flops 944332800 | bytes 3637248 | tf_op jit(solution)/shard_map/dot_general | solution.py:189
  86.8 2.8 %pick_views.9 = bf16[3,200,768]{2,1,0:T(8,128)(2,1)} custom-call(s32[3]{0:T(128)} %get-tuple-element.9.index, bf16[4,200,768]{2,1,0:T(8,128)(2,1)} %collective-permute-done.6.source.refs_5_), custom_call_target="tpu_custom_call" | custom-call | tf_op jit(solution)/shard_map/pick_views/pallas_call | solution.py:147
  89.6 2.9 %pick_views.8 = bf16[3,200,768]{2,1,0:T(8,128)(2,1)} custom-call(s32[3]{0:T(128)} %get-tuple-element.10.index, bf16[4,200,768]{2,1,0:T(8,128)(2,1)} %collective-permute-done.2.source.refs_4_), custom_call_target="tpu_custom_call" | custom-call | tf_op jit(solution)/shard_map/pick_views/pallas_call | solution.py:147
  92.5 1.6 collective-permute-start.10
  94.1 2.4 %collective-permute-start.9 = (bf16[3,200,768]{2,1,0:T(8,128)(2,1)}, bf16[3,200,768]{2,1,0:T(8,128)(2,1)}, u32[]{:S(2)}, u32[]{:S(2)}) collective-permute-start(bf16[3,200,768]{2,1,0:T(8,128)(2,1)} %pick_views.8), channel_id=1, source_target_pairs={{4,5},{5,4},{6,7},{7,6},{12,13},{13,12},{14,15},{15,14},{20,21},{2... | collective-permute-start | bytes 2764808 | tf_op jit(solution)/shard_map/ppermute | solution.py:251
  97.1 2.8 %pick_views.6 = bf16[3,200,768]{2,1,0:T(8,128)(2,1)} custom-call(s32[3]{0:T(128)} %get-tuple-element.12.index, bf16[4,200,768]{2,1,0:T(8,128)(2,1)} %collective-permute-done.3.source.refs_4_), custom_call_target="tpu_custom_call" | custom-call | tf_op jit(solution)/shard_map/pick_views/pallas_call | solution.py:147
  99.9 2.9 %pick_views.7 = bf16[3,200,768]{2,1,0:T(8,128)(2,1)} custom-call(s32[3]{0:T(128)} %get-tuple-element.11.index, bf16[4,200,768]{2,1,0:T(8,128)(2,1)} %collective-permute-done.7.source.refs_5_), custom_call_target="tpu_custom_call" | custom-call | tf_op jit(solution)/shard_map/pick_views/pallas_call | solution.py:147
  102.9 0.7 collective-permute-start.4
  103.6 0.9 collective-permute-start.8
  104.5 16.4 %attend_phase.4.refs_10_ = f32[4,196,768]{2,1,0:T(8,128)} custom-call(s32[3,18]{1,0:T(4,128)} %pad_add_fusion.refs_0_, bf16[4,200,768]{2,1,0:T(8,128)(2,1)} %bitcast.17, bf16[768,768]{1,0:T(8,128)(2,1)} %refs_2_.7, bf16[768,768]{1,0:T(8,128)(2,1)} %refs_3_.7, bf16[4,200,768]{2,1,0:T(8,128)(2,1)} %collective-permute-done.1.source.refs_4_, ...), custom_call_target="tpu_custom_call" | custom-call | flops 3737911296 | bytes 4816896 | tf_op jit(solution)/shard_map/attend_phase/pallas_call | solution.py:113
  120.9 23.0 %attend_phase.5.refs_8_ = f32[4,196,768]{2,1,0:T(8,128)} custom-call(s32[3,18]{1,0:T(4,128)} %pad_add_fusion.refs_0_, bf16[4,200,768]{2,1,0:T(8,128)(2,1)} %bitcast.18, bf16[768,768]{1,0:T(8,128)(2,1)} %refs_2_.7, bf16[768,768]{1,0:T(8,128)(2,1)} %refs_3_.7, bf16[4,200,768]{2,1,0:T(8,128)(2,1)} %collective-permute-done.2.source.refs_4_, ...), custom_call_target="tpu_custom_call" | custom-call | flops 3737911296 | bytes 4816896 | tf_op jit(solution)/shard_map/attend_phase/pallas_call | solution.py:113
  143.9 12.1 %attend_phase.6.refs_6_ = f32[4,196,768]{2,1,0:T(8,128)} custom-call(s32[3,18]{1,0:T(4,128)} %pad_add_fusion.refs_0_, bf16[4,200,768]{2,1,0:T(8,128)(2,1)} %bitcast.19, bf16[768,768]{1,0:T(8,128)(2,1)} %refs_2_.7, bf16[768,768]{1,0:T(8,128)(2,1)} %refs_3_.7, bf16[4,200,768]{2,1,0:T(8,128)(2,1)} %collective-permute-done.3.source.refs_4_, ...), custom_call_target="tpu_custom_call" | custom-call | flops 3737911296 | bytes 4816896 | tf_op jit(solution)/shard_map/attend_phase/pallas_call | solution.py:113
  156.0 0.9 copy-done.5
  156.9 1.0 copy-done.6
  157.9 7.2 %attend_phase.7 = bf16[4,196,768]{2,1,0:T(8,128)(2,1)} custom-call(s32[3,18]{1,0:T(4,128)} %pad_add_fusion.refs_0_, bf16[4,200,768]{2,1,0:T(8,128)(2,1)} %bitcast.20, bf16[768,768]{1,0:T(8,128)(2,1)} %refs_2_.7, bf16[768,768]{1,0:T(8,128)(2,1)} %refs_3_.7, bf16[3,200,768]{2,1,0:T(8,128)(2,1)} %copy-done.5, bf16[3,200,768]{2,1,0:T(8,128)(2,1)} %copy-done.6, ...), custom_call_target="tpu_custom_call" | custom-call | flops 3737911296 | bytes 4816896 | tf_op jit(solution)/shard_map/attend_phase/pallas_call | solution.py:113
  165.1 2.8 %copy.15 = bf16[4,196,768]{2,0,1:T(4,128)(2,1)} copy(bf16[4,196,768]{2,1,0:T(8,128)(2,1)} %attend_phase.7) | data formatting | bytes 2408448 | tf_op jit(solution)/shard_map/attend_phase/pallas_call | solution.py:113
  (57 shorter events, 4.1 us)
Async XLA Ops:
  0.0 84.6 %copy-start = (bf16[768,768]{1,0:T(8,128)(2,1)S(1)}, bf16[768,768]{1,0:T(8,128)(2,1)}, u32[]{:S(2)}) copy-start(bf16[768,768]{1,0:T(8,128)(2,1)} %param.10) | copy-start | bytes 3538948
  1.5 7.6 %copy-start.4 = (s32[4,4]{1,0:T(4,128)S(1)}, s32[4,4]{1,0:T(4,128)}, u32[]{:S(2)}) copy-start(s32[4,4]{1,0:T(4,128)} %param.14) | copy-start | bytes 196
  1.5 7.7 %copy-start.9 = (s32[4]{0:T(128)S(1)}, s32[4]{0:T(128)}, u32[]{:S(2)}) copy-start(s32[4]{0:T(128)} %param.15) | copy-start | bytes 52
  2.7 31.0 %collective-permute-start.1 = (bf16[4,200,768]{2,1,0:T(8,128)(2,1)}, bf16[4,200,768]{2,1,0:T(8,128)(2,1)}, u32[]{:S(2)}, u32[]{:S(2)}) collective-permute-start(bf16[4,200,768]{2,1,0:T(8,128)(2,1)} %pad.6.refs_8_), channel_id=1, source_target_pairs={{0,2},{1,3},{2,4},{3,5},{4,6},{5,7},{8,10},{9,11},{10,12},{11,13},... | collective-permute-start | bytes 3686408 | tf_op jit(solution)/shard_map/ppermute | solution.py:243
  6.2 31.0 %collective-permute-start.5 = (bf16[4,200,768]{2,1,0:T(8,128)(2,1)}, bf16[4,200,768]{2,1,0:T(8,128)(2,1)}, u32[]{:S(2)}, u32[]{:S(2)}) collective-permute-start(bf16[4,200,768]{2,1,0:T(8,128)(2,1)} %pad.6.refs_8_), channel_id=1, source_target_pairs={{2,0},{3,1},{4,2},{5,3},{6,4},{7,5},{10,8},{11,9},{12,10},{13,11},... | collective-permute-start | bytes 3686408 | tf_op jit(solution)/shard_map/ppermute | solution.py:243
  8.5 94.3 %collective-permute-start.15 = (bf16[4,200,768]{2,1,0:T(8,128)(2,1)}, bf16[4,200,768]{2,1,0:T(8,128)(2,1)}, u32[]{:S(2)}, u32[]{:S(2)}) collective-permute-start(bf16[4,200,768]{2,1,0:T(8,128)(2,1)} %pad.6.refs_8_), channel_id=1, source_target_pairs={{0,1},{1,0},{2,3},{3,2},{4,5},{5,4},{6,7},{7,6},{8,9},{9,8},{10,11... | collective-permute-start | bytes 3686408 | tf_op jit(solution)/shard_map/ppermute | solution.py:275
  33.6 30.1 %collective-permute-start.2 = (bf16[4,200,768]{2,1,0:T(8,128)(2,1)}, bf16[4,200,768]{2,1,0:T(8,128)(2,1)}, u32[]{:S(2)}, u32[]{:S(2)}) collective-permute-start(bf16[4,200,768]{2,1,0:T(8,128)(2,1)} %collective-permute-done.1.source.refs_4_), channel_id=1, source_target_pairs={{2,4},{3,5},{4,6},{5,7},{10,12},{11,13},{12,14},{13,15},{18,20},{1... | collective-permute-start | bytes 3686408 | tf_op jit(solution)/shard_map/ppermute | solution.py:243
  37.1 31.1 %collective-permute-start.6 = (bf16[4,200,768]{2,1,0:T(8,128)(2,1)}, bf16[4,200,768]{2,1,0:T(8,128)(2,1)}, u32[]{:S(2)}, u32[]{:S(2)}) collective-permute-start(bf16[4,200,768]{2,1,0:T(8,128)(2,1)} %collective-permute-done.5.source.refs_5_), channel_id=1, source_target_pairs={{2,0},{3,1},{4,2},{5,3},{10,8},{11,9},{12,10},{13,11},{18,16},{19,... | collective-permute-start | bytes 3686408 | tf_op jit(solution)/shard_map/ppermute | solution.py:243
  41.8 28.2 %collective-permute-start = (s32[4,3]{0,1:T(4,128)S(1)}, s32[4,3]{0,1:T(4,128)S(1)}, u32[]{:S(2)}, u32[]{:S(2)}) collective-permute-start(s32[4,3]{0,1:T(4,128)S(1)} %select_reduce_fusion), channel_id=1, source_target_pairs={{0,1},{1,0},{2,3},{3,2},{4,5},{5,4},{6,7},{7,6},{8,9},{9,8},{10,11... | collective-permute-start | bytes 152 | tf_op jit(solution)/shard_map/ppermute | solution.py:259
  43.1 30.6 %collective-permute-start.13 = (bf16[1,200,768]{2,1,0:T(8,128)(2,1)S(1)}, bf16[1,200,768]{2,1,0:T(8,128)(2,1)S(1)}, u32[]{:S(2)}, u32[]{:S(2)}) collective-permute-start(bf16[1,200,768]{2,1,0:T(8,128)(2,1)S(1)} %constant_dynamic-slice_fusion), channel_id=1, source_target_pairs={{0,8},{8,16},{16,24},{24,0},{1,9},{9,17},{17,25},{25,1},{2,10},{10... | collective-permute-start | bytes 921608 | tf_op jit(solution)/shard_map/ppermute | solution.py:184
  44.0 32.2 %copy-start.10 = (s32[2]{0:T(128)S(1)}, s32[2]{0:T(128)}, u32[]{:S(2)}) copy-start(s32[2]{0:T(128)} %constant.142.clone) | copy-start | bytes 28
  63.7 28.7 %collective-permute-start.3 = (bf16[4,200,768]{2,1,0:T(8,128)(2,1)}, bf16[4,200,768]{2,1,0:T(8,128)(2,1)}, u32[]{:S(2)}, u32[]{:S(2)}) collective-permute-start(bf16[4,200,768]{2,1,0:T(8,128)(2,1)} %collective-permute-done.2.source.refs_4_), channel_id=1, source_target_pairs={{4,6},{5,7},{12,14},{13,15},{20,22},{21,23},{28,30},{29,31}} | collective-permute-start | bytes 3686408 | tf_op jit(solution)/shard_map/ppermute | solution.py:243
  68.3 25.8 %collective-permute-start.7 = (bf16[4,200,768]{2,1,0:T(8,128)(2,1)}, bf16[4,200,768]{2,1,0:T(8,128)(2,1)}, u32[]{:S(2)}, u32[]{:S(2)}) collective-permute-start(bf16[4,200,768]{2,1,0:T(8,128)(2,1)} %collective-permute-done.6.source.refs_5_), channel_id=1, source_target_pairs={{2,0},{3,1},{10,8},{11,9},{18,16},{19,17},{26,24},{27,25}} | collective-permute-start | bytes 3686408 | tf_op jit(solution)/shard_map/ppermute | solution.py:243
  70.0 10.5 %collective-permute-start.14 = (bf16[1,200,768]{2,1,0:T(8,128)(2,1)S(1)}, bf16[1,200,768]{2,1,0:T(8,128)(2,1)S(1)}, u32[]{:S(2)}, u32[]{:S(2)}) collective-permute-start(bf16[1,200,768]{2,1,0:T(8,128)(2,1)S(1)} %constant_dynamic-slice_fusion), channel_id=1, source_target_pairs={{8,0},{16,8},{24,16},{0,24},{9,1},{17,9},{25,17},{1,25},{10,2},{18... | collective-permute-start | bytes 921608 | tf_op jit(solution)/shard_map/ppermute | solution.py:185
  73.7 3.9 %copy-start.7 = (bf16[1,200,768]{2,1,0:T(8,128)(2,1)}, bf16[1,200,768]{2,1,0:T(8,128)(2,1)S(1)}, u32[]{:S(2)}) copy-start(bf16[1,200,768]{2,1,0:T(8,128)(2,1)S(1)} %collective-permute-done.13.refs_8_) | copy-start | bytes 921604
  73.7 29.9 %collective-permute-start.11 = (bf16[3,200,768]{2,1,0:T(8,128)(2,1)}, bf16[3,200,768]{2,1,0:T(8,128)(2,1)}, u32[]{:S(2)}, u32[]{:S(2)}) collective-permute-start(bf16[3,200,768]{2,1,0:T(8,128)(2,1)} %pick_views.10), channel_id=1, source_target_pairs={{2,3},{3,2},{4,5},{5,4},{6,7},{7,6},{10,11},{11,10},{12,13},{13,12... | collective-permute-start | bytes 2764808 | tf_op jit(solution)/shard_map/ppermute | solution.py:251
  77.7 7.0 %copy-start.1 = (bf16[4,200,768]{2,1,0:T(8,128)(2,1)S(1)}, bf16[4,200,768]{2,1,0:T(8,128)(2,1)}, u32[]{:S(2)}) copy-start(bf16[4,200,768]{2,1,0:T(8,128)(2,1)} %fusion.3) | copy-start | bytes 3686404
  80.6 6.2 %copy-start.8 = (bf16[1,200,768]{2,1,0:T(8,128)(2,1)}, bf16[1,200,768]{2,1,0:T(8,128)(2,1)S(1)}, u32[]{:S(2)}) copy-start(bf16[1,200,768]{2,1,0:T(8,128)(2,1)S(1)} %collective-permute-done.14.refs_9_) | copy-start | bytes 921604
  80.6 40.3 %collective-permute-start.12 = (bf16[3,200,768]{2,1,0:T(8,128)(2,1)}, bf16[3,200,768]{2,1,0:T(8,128)(2,1)}, u32[]{:S(2)}, u32[]{:S(2)}) collective-permute-start(bf16[3,200,768]{2,1,0:T(8,128)(2,1)} %pick_views.11), channel_id=1, source_target_pairs={{0,1},{1,0},{2,3},{3,2},{4,5},{5,4},{8,9},{9,8},{10,11},{11,10},{1... | collective-permute-start | bytes 2764808 | tf_op jit(solution)/shard_map/ppermute | solution.py:251
  89.6 2.9 %copy-start.2 = (bf16[3,200,768]{2,1,0:T(8,128)(2,1)S(1)}, bf16[3,200,768]{2,1,0:T(8,128)(2,1)}, u32[]{:S(2)}) copy-start(bf16[3,200,768]{2,1,0:T(8,128)(2,1)} %pick_views.9) | copy-start | bytes 2764804
  92.5 51.4 %collective-permute-start.10 = (bf16[3,200,768]{2,1,0:T(8,128)(2,1)S(1)}, bf16[3,200,768]{2,1,0:T(8,128)(2,1)}, u32[]{:S(2)}, u32[]{:S(2)}) collective-permute-start(bf16[3,200,768]{2,1,0:T(8,128)(2,1)S(1)} %copy-done.2), channel_id=1, source_target_pairs={{0,1},{1,0},{2,3},{3,2},{8,9},{9,8},{10,11},{11,10},{16,17},{17,16... | collective-permute-start | bytes 2764808 | tf_op jit(solution)/shard_map/ppermute | solution.py:251
  94.1 49.8 %collective-permute-start.9 = (bf16[3,200,768]{2,1,0:T(8,128)(2,1)}, bf16[3,200,768]{2,1,0:T(8,128)(2,1)}, u32[]{:S(2)}, u32[]{:S(2)}) collective-permute-start(bf16[3,200,768]{2,1,0:T(8,128)(2,1)} %pick_views.8), channel_id=1, source_target_pairs={{4,5},{5,4},{6,7},{7,6},{12,13},{13,12},{14,15},{15,14},{20,21},{2... | collective-permute-start | bytes 2764808 | tf_op jit(solution)/shard_map/ppermute | solution.py:251
  99.9 3.0 %copy-start.3 = (bf16[3,200,768]{2,1,0:T(8,128)(2,1)S(1)}, bf16[3,200,768]{2,1,0:T(8,128)(2,1)}, u32[]{:S(2)}) copy-start(bf16[3,200,768]{2,1,0:T(8,128)(2,1)} %pick_views.6) | copy-start | bytes 2764804
  102.9 53.1 %collective-permute-start.4 = (bf16[3,200,768]{2,1,0:T(8,128)(2,1)S(1)}, bf16[3,200,768]{2,1,0:T(8,128)(2,1)S(1)}, u32[]{:S(2)}, u32[]{:S(2)}) collective-permute-start(bf16[3,200,768]{2,1,0:T(8,128)(2,1)S(1)} %copy-done.3), channel_id=1, source_target_pairs={{6,7},{7,6},{14,15},{15,14},{22,23},{23,22},{30,31},{31,30}} | collective-permute-start | bytes 2764808 | tf_op jit(solution)/shard_map/ppermute | solution.py:251
  103.6 52.4 %collective-permute-start.8 = (bf16[3,200,768]{2,1,0:T(8,128)(2,1)}, bf16[3,200,768]{2,1,0:T(8,128)(2,1)S(1)}, u32[]{:S(2)}, u32[]{:S(2)}) collective-permute-start(bf16[3,200,768]{2,1,0:T(8,128)(2,1)} %pick_views.7), channel_id=1, source_target_pairs={{0,1},{1,0},{8,9},{9,8},{16,17},{17,16},{24,25},{25,24}} | collective-permute-start | bytes 2764808 | tf_op jit(solution)/shard_map/ppermute | solution.py:251
  156.0 0.9 copy-start.5
  156.9 1.0 copy-start.6
